TPU v7x, 32 devices: a whole 2x2x4 slice. The times are simulated.
32 devices in a mesh: dp: 4 (over z), tensor: 8 (over y, x, core).
Axes of the slice: x: 2, y: 2, z: 4, core: 2. Of those that a mesh axis runs over, the one named last changes fastest.
Arguments:
- tokens: bfloat16 [8192, 1152], P('dp'), may hold values from -6 to 6
- condition: float32 [32, 1152], P('dp'), may hold values from -6 to 6
- timesteps: int32 [32], P('dp'), may hold values from 0 to 999
- route_masks: int32 [1000, 16, 2], P(None, 'tensor'), may hold values 0 or 1
- modulate_weight: bfloat16 [1152, 6, 1152], P(None, None, 'tensor'), may hold values from -0.1875 to 0.1875
- modulate_bias: bfloat16 [6, 1152], P(None, 'tensor'), may hold values from -1.5 to 1.5
- input_weight: bfloat16 [1152, 3, 1152], P(None, None, 'tensor'), may hold values from -0.1875 to 0.1875
- input_bias: bfloat16 [2, 1152], P(None, 'tensor'), may hold values from -1.5 to 1.5
- output_weight: bfloat16 [1152, 1152], P('tensor'), may hold values from -1.5 to 1.5
- output_bias: bfloat16 [1152], replicated, may hold values from -1.5 to 1.5
- expand_weight: bfloat16 [1152, 4608], P(None, 'tensor'), may hold values from -0.1875 to 0.1875
- expand_bias: bfloat16 [4608], P('tensor'), may hold values from -1.5 to 1.5
- reduce_weight: bfloat16 [4608, 1152], P('tensor'), may hold values from -0.1875 to 0.1875
- reduce_bias: bfloat16 [1152], replicated, may hold values from -1.5 to 1.5
- router_weight: bfloat16 [1152, 16, 2], P(None, 'tensor'), may hold values from -0.1875 to 0.1875
- router_bias: bfloat16 [16, 2], P('tensor'), may hold values from -1.2 to 1.2
- out_cotangent: bfloat16 [8192, 1152], P('dp'), may hold values from -6 to 6
Outputs:
- block_output: float32 [8192, 1152], P('dp')
- tokens_grad: float32 [8192, 1152], P('dp')
- modulate_weight_grad: float32 [1152, 6, 1152], P(None, None, 'tensor')
- modulate_bias_grad: float32 [6, 1152], P(None, 'tensor')
- input_weight_grad: float32 [1152, 3, 1152], P(None, None, 'tensor')
- input_bias_grad: float32 [2, 1152], P(None, 'tensor')
- output_weight_grad: float32 [1152, 1152], P('tensor')
- output_bias_grad: float32 [1152], replicated
- expand_weight_grad: float32 [1152, 4608], P(None, 'tensor')
- expand_bias_grad: float32 [4608], P('tensor')
- reduce_weight_grad: float32 [4608, 1152], P('tensor')
- reduce_bias_grad: float32 [1152], replicated
- router_weight_grad: float32 [1152, 16, 2], P(None, 'tensor')
- router_bias_grad: float32 [16, 2], P('tensor')
Inputs may be any that keep to these rules, and one draw needn't show every extreme that they name: `timesteps`: each timestep selects the row of route_masks used by its item.
All inputs are finite; a program needn't handle non-finite values. No bound on the sum of `route_masks` on one device may be relied on, other than what follows from the above.
Results may differ from a plain program's by a relative error of at most 0.013.
The roundings to bfloat16 on the way count: a program that leaves them out, or rounds other values in their place, can miss the bound.
Values may be sent and summed in bfloat16 or wider, within the bound.
A program may use at most 256 MiB of HBM per device.

v0:
```python
import math
import jax
import jax.numpy as jnp
from jax import lax
from jax.sharding import PartitionSpec as P

HIGHEST = lax.Precision.HIGHEST
EPSILON = 1e-06


def layer_norm(values):
    center = values - jnp.mean(values, axis=-1, keepdims=True)
    inverse = lax.rsqrt(jnp.mean(center * center, axis=-1, keepdims=True) + EPSILON)
    return (center * inverse, inverse)


def norm_back(grad_norm, normed, inverse):
    mean_grad = jnp.mean(grad_norm, axis=-1, keepdims=True)
    mean_cross = jnp.mean(grad_norm * normed, axis=-1, keepdims=True)
    return inverse * (grad_norm - mean_grad - normed * mean_cross)


def gelu_tanh(values):
    return jax.nn.gelu(values, approximate=True)


def contract_rows(left, right):
    return lax.dot_general(
        left, right, (((0,), (0,)), ((), ())), preferred_element_type=jnp.float32
    )


def contract_cols(left, right):
    return lax.dot_general(
        left, right, (((1,), (1,)), ((), ())), preferred_element_type=jnp.float32
    )


def body(
    tokens,
    condition,
    timesteps,
    route_masks,
    modulate_weight,
    modulate_bias,
    input_weight,
    input_bias,
    output_weight,
    output_bias,
    expand_weight,
    expand_bias,
    reduce_weight,
    reduce_bias,
    router_weight,
    router_bias,
    out_cotangent,
):
    model_width = tokens.shape[1]
    item_count = condition.shape[0]
    rows_all = tokens.shape[0]
    item_length = rows_all // item_count
    local_heads = router_weight.shape[1]
    local_width = input_weight.shape[2]
    head_size = local_width // local_heads
    group_width = expand_weight.shape[1] // local_heads
    score_scale = 1.0 / math.sqrt(head_size)
    silu_condition = jax.nn.silu(condition).astype(jnp.bfloat16)
    condition_low = condition.astype(jnp.bfloat16)
    modulate_part = jnp.einsum(
        "bd,dke->bke", silu_condition, modulate_weight, preferred_element_type=jnp.float32
    ) + modulate_bias.astype(jnp.float32)
    modulation = lax.all_gather(modulate_part, "tensor", axis=2, tiled=True)
    shift_one, scale_one, gate_one, shift_two, scale_two, gate_two = [
        modulation[:, column][:, None, :] for column in range(6)
    ]
    logits = jnp.einsum(
        "bd,dhc->bhc", condition_low, router_weight, preferred_element_type=jnp.float32
    ) + router_bias.astype(jnp.float32)
    sigmoid_out = jax.nn.sigmoid(logits)
    step_table = (
        timesteps[:, None] == jnp.arange(route_masks.shape[0], dtype=jnp.int32)[None, :]
    ).astype(jnp.float32)
    mask_rows = jnp.einsum(
        "bs,shc->bhc", step_table, route_masks.astype(jnp.float32), precision=HIGHEST
    )
    gate_values = mask_rows * sigmoid_out
    head_gate = gate_values[:, :, 0]
    group_gate = gate_values[:, :, 1]
    inputs_f = tokens.astype(jnp.float32).reshape(item_count, item_length, model_width)
    normed_one, inverse_one = layer_norm(inputs_f)
    hidden_one = (normed_one * (1.0 + scale_one) + shift_one).astype(jnp.bfloat16)
    projected = jnp.einsum(
        "bsd,dke->bske", hidden_one, input_weight, preferred_element_type=jnp.float32
    )
    input_bias_f = input_bias.astype(jnp.float32)
    head_shape = (item_count, item_length, local_heads, head_size)
    queries = (projected[:, :, 0] + input_bias_f[0]).astype(jnp.bfloat16).reshape(head_shape)
    keys_low = projected[:, :, 1].astype(jnp.bfloat16).reshape(head_shape)
    values_low = (projected[:, :, 2] + input_bias_f[1]).astype(jnp.bfloat16).reshape(head_shape)
    scores = (
        jnp.einsum("bqhe,bkhe->bhqk", queries, keys_low, preferred_element_type=jnp.float32)
        * score_scale
    )
    row_max = jnp.max(scores, axis=-1, keepdims=True)
    log_total = row_max + jnp.log(jnp.sum(jnp.exp(scores - row_max), axis=-1, keepdims=True))
    softmax_low = jnp.exp(scores - log_total).astype(jnp.bfloat16)
    mixed_heads = jnp.einsum(
        "bhqk,bkhe->bqhe", softmax_low, values_low, preferred_element_type=jnp.float32
    )
    gated_heads = (
        (mixed_heads * head_gate[:, None, :, None])
        .astype(jnp.bfloat16)
        .reshape(rows_all, local_width)
    )
    attention_part = jnp.dot(gated_heads, output_weight, preferred_element_type=jnp.float32)
    attention = (lax.psum(attention_part, "tensor") + output_bias.astype(jnp.float32)).reshape(
        item_count, item_length, model_width
    )
    residual_one = inputs_f + gate_one * attention
    normed_two, inverse_two = layer_norm(residual_one)
    hidden_two = (
        (normed_two * (1.0 + scale_two) + shift_two)
        .astype(jnp.bfloat16)
        .reshape(rows_all, model_width)
    )
    expanded = jnp.dot(
        hidden_two, expand_weight, preferred_element_type=jnp.float32
    ) + expand_bias.astype(jnp.float32)
    activated = gelu_tanh(expanded)
    group_shape = (item_count, item_length, local_heads, group_width)
    gated_channels = (
        (activated.reshape(group_shape) * group_gate[:, None, :, None])
        .astype(jnp.bfloat16)
        .reshape(rows_all, -1)
    )
    mlp_part = jnp.dot(gated_channels, reduce_weight, preferred_element_type=jnp.float32)
    branch_two = (lax.psum(mlp_part, "tensor") + reduce_bias.astype(jnp.float32)).reshape(
        item_count, item_length, model_width
    )
    block_output = residual_one + gate_two * branch_two
    cotangent = out_cotangent.astype(jnp.float32).reshape(item_count, item_length, model_width)
    gate_two_grad = jnp.sum(cotangent * branch_two, axis=1)
    branch_grad = (gate_two * cotangent).astype(jnp.bfloat16).reshape(rows_all, model_width)
    reduce_bias_grad = jnp.sum(branch_grad.astype(jnp.float32), axis=0)
    reduce_weight_grad = contract_rows(gated_channels, branch_grad)
    channel_blocks = contract_cols(branch_grad, reduce_weight).reshape(group_shape)
    group_gate_grad = jnp.sum(channel_blocks * activated.reshape(group_shape), axis=(1, 3))
    activated_grad = (channel_blocks * group_gate[:, None, :, None]).reshape(rows_all, -1)
    expanded_grad = jax.vjp(gelu_tanh, expanded)[1](activated_grad)[0].astype(jnp.bfloat16)
    expand_bias_grad = jnp.sum(expanded_grad.astype(jnp.float32), axis=0)
    expand_weight_grad = contract_rows(hidden_two, expanded_grad)
    hidden_two_part = contract_cols(expanded_grad, expand_weight)
    hidden_two_grad = lax.psum(hidden_two_part, "tensor").reshape(
        item_count, item_length, model_width
    )
    shift_two_grad = jnp.sum(hidden_two_grad, axis=1)
    scale_two_grad = jnp.sum(hidden_two_grad * normed_two, axis=1)
    residual_grad = cotangent + norm_back(
        hidden_two_grad * (1.0 + scale_two), normed_two, inverse_two
    )
    branch_one_grad = (gate_one * residual_grad).astype(jnp.bfloat16).reshape(rows_all, model_width)
    output_bias_grad = jnp.sum(branch_one_grad.astype(jnp.float32), axis=0)
    output_weight_grad = contract_rows(gated_heads, branch_one_grad)
    heads_grad = contract_cols(branch_one_grad, output_weight).reshape(head_shape)
    head_gate_grad = jnp.sum(heads_grad * mixed_heads, axis=(1, 3))
    mixed_grad = (heads_grad * head_gate[:, None, :, None]).astype(jnp.bfloat16)
    scores_again = (
        jnp.einsum("bqhe,bkhe->bhqk", queries, keys_low, preferred_element_type=jnp.float32)
        * score_scale
    )
    softmax_full = jnp.exp(scores_again - log_total)
    softmax_grad = jnp.einsum(
        "bqhe,bkhe->bhqk", mixed_grad, values_low, preferred_element_type=jnp.float32
    )
    values_grad = jnp.einsum(
        "bhqk,bqhe->bkhe",
        softmax_full.astype(jnp.bfloat16),
        mixed_grad,
        preferred_element_type=jnp.float32,
    )
    score_grad = (
        softmax_full * (softmax_grad - jnp.sum(softmax_grad * softmax_full, axis=-1, keepdims=True))
    ).astype(jnp.bfloat16)
    queries_grad = (
        jnp.einsum("bhqk,bkhe->bqhe", score_grad, keys_low, preferred_element_type=jnp.float32)
        * score_scale
    )
    keys_grad = (
        jnp.einsum("bhqk,bqhe->bkhe", score_grad, queries, preferred_element_type=jnp.float32)
        * score_scale
    )
    stacked_grad = (
        jnp.stack([queries_grad, keys_grad, values_grad], axis=2)
        .reshape(item_count, item_length, 3, local_width)
        .astype(jnp.bfloat16)
    )
    stacked_f = stacked_grad.astype(jnp.float32)
    input_bias_grad = jnp.stack(
        [jnp.sum(stacked_f[:, :, 0], axis=(0, 1)), jnp.sum(stacked_f[:, :, 2], axis=(0, 1))]
    )
    input_weight_grad = jnp.einsum(
        "bsd,bske->dke", hidden_one, stacked_grad, preferred_element_type=jnp.float32
    )
    hidden_one_part = jnp.einsum(
        "bske,dke->bsd", stacked_grad, input_weight, preferred_element_type=jnp.float32
    ).reshape(rows_all, model_width)
    hidden_one_grad = lax.psum(hidden_one_part, "tensor")
    gate_one_grad = jnp.sum(residual_grad * attention, axis=1)
    hidden_one_grad = hidden_one_grad.reshape(item_count, item_length, model_width)
    shift_one_grad = jnp.sum(hidden_one_grad, axis=1)
    scale_one_grad = jnp.sum(hidden_one_grad * normed_one, axis=1)
    tokens_grad = residual_grad + norm_back(
        hidden_one_grad * (1.0 + scale_one), normed_one, inverse_one
    )
    modulation_grad = jnp.stack(
        [
            shift_one_grad,
            scale_one_grad,
            gate_one_grad,
            shift_two_grad,
            scale_two_grad,
            gate_two_grad,
        ],
        axis=1,
    )
    column_start = lax.axis_index("tensor") * modulate_weight.shape[2]
    own_grad = lax.dynamic_slice_in_dim(modulation_grad, column_start, modulate_weight.shape[2], 2)
    modulate_weight_grad = jnp.einsum(
        "bd,bke->dke", silu_condition.astype(jnp.float32), own_grad, precision=HIGHEST
    )
    modulate_bias_grad = jnp.sum(own_grad, axis=0)
    gate_grad = jnp.stack([head_gate_grad, group_gate_grad], axis=-1)
    logit_grad = gate_grad * mask_rows * sigmoid_out * (1.0 - sigmoid_out)
    router_weight_grad = jnp.einsum(
        "bd,bhc->dhc", condition_low.astype(jnp.float32), logit_grad, precision=HIGHEST
    )
    router_bias_grad = jnp.sum(logit_grad, axis=0)
    summed = lax.psum(
        (
            modulate_weight_grad,
            modulate_bias_grad,
            input_weight_grad,
            input_bias_grad,
            output_weight_grad,
            output_bias_grad,
            expand_weight_grad,
            expand_bias_grad,
            reduce_weight_grad,
            reduce_bias_grad,
            router_weight_grad,
            router_bias_grad,
        ),
        "dp",
    )
    return (
        block_output.reshape(rows_all, model_width),
        tokens_grad.reshape(rows_all, model_width),
    ) + tuple(summed)


def solution(mesh):
    return jax.shard_map(
        body,
        mesh=mesh,
        in_specs=(
            P("dp", None),
            P("dp", None),
            P("dp"),
            P(None, "tensor", None),
            P(None, None, "tensor"),
            P(None, "tensor"),
            P(None, None, "tensor"),
            P(None, "tensor"),
            P("tensor", None),
            P(),
            P(None, "tensor"),
            P("tensor"),
            P("tensor", None),
            P(),
            P(None, "tensor", None),
            P("tensor", None),
            P("dp", None),
        ),
        out_specs=(
            P("dp", None),
            P("dp", None),
            P(None, None, "tensor"),
            P(None, "tensor"),
            P(None, None, "tensor"),
            P(None, "tensor"),
            P("tensor", None),
            P(),
            P(None, "tensor"),
            P("tensor"),
            P("tensor", None),
            P(),
            P(None, "tensor", None),
            P("tensor", None),
        ),
        check_vma=False,
    )
```

profile of v0, /device:TPU:0, one launch (start us, length us, event | category | flops | bytes accessed | tf_op | source)
XLA Modules:
  0.0 1134.2 jit_solution(17159783250025493048)
XLA Ops:
  7.3 3.2 convert_reduce_fusion.2
  10.5 3.7 multiply_reduce_fusion.5
  15.8 29.1 %all_gather.3 = f32[8,6,1152]{1,0,2:T(8,128)} all-gather(f32[8,6,144]{1,0,2:T(8,128)S(1)} %copy.78), channel_id=1, replica_groups=mesh['dp'=4,'tensor'=8] {'tensor'}, dimensions={2}, use_global_device_ids=true | all-gather | bytes 248832 | tf_op jit(solution)/shard_map/all_gather | solution.py:72
  44.9 22.1 %fusion.64 = (f32[8,1,1152]{1,0,2:T(8,128)}, f32[8,1,1152]{1,0,2:T(8,128)}, f32[8,1,1152]{1,0,2:T(8,128)}, f32[8,1,1152]{1,0,2:T(8,128)}, f32[8,1,1152]{1,0,2:T(8,128)}, /*index=5*/f32[8,1,1152]{1,0,2:T(8,128)}) fusion(f32[8,6,1152]{1,0,2:T(8,128)} %all_gather.3), kind=kLoop, calls=%fused_computation.135 | loop fusion | bytes 442368 | tf_op jit(solution)/shard_map/slice | solution.py:74
  67.0 3.4 copy.114
  70.4 3.3 copy.113
  73.8 4.9 fusion.17
  82.3 2.0 multiply_convert_fusion.3
  84.7 5.3 fusion.70
  91.1 4.4 copy.121
  95.5 3.6 copy.116
  99.2 3.3 copy.115
  102.5 3.4 copy.112
  105.9 3.4 copy.117
  109.3 4.5 convert_reduce_fusion
  113.9 5.1 broadcast_multiply_fusion
  119.0 2.7 copy.90
  121.7 4.4 copy.122
  126.1 102.3 %all-reduce.8.cloned.1.call-done = f32[2048,1152]{1,0:T(8,128)} async-done(((f32[2048,1152]{1,0:T(8,128)}), f32[2048,1152]{1,0:T(8,128)}) %all-reduce.8.cloned.1.call-update) | async-done | bytes 9437200 | tf_op jit(solution)/shard_map/psum | solution.py:116
  228.4 10.4 fusion.62
  238.8 4.9 multiply_reduce_fusion.4
  245.1 2.2 fusion.5
  248.4 8.9 multiply_convert_fusion
  258.6 7.0 fusion.72
  265.7 9.8 fusion.71
  275.6 128.3 %all-reduce.10.cloned.1.call-done = f32[2048,1152]{1,0:T(8,128)} async-done(((f32[2048,1152]{1,0:T(8,128)}), f32[2048,1152]{1,0:T(8,128)}) %all-reduce.10.cloned.1.call-update) | async-done | bytes 9437200 | tf_op jit(solution)/shard_map/psum | solution.py:153
  403.8 8.1 fusion.9
  412.9 10.7 convert_reduce_fusion.1
  423.6 2.6 multiply_reduce_fusion.8
  432.4 2.1 fusion.55
  434.7 5.4 convolution_bitcast_fusion
  440.8 7.9 fusion.75
  448.7 4.7 fusion.74
  453.5 4.3 fusion.73
  457.8 6.6 fusion.22
  464.4 215.9 %all-reduce.12.cloned.1.call-done = (f32[2048,1152]{1,0:T(8,128)}, f32[2048,1152]{1,0:T(8,128)}) async-done(((f32[2048,1152]{1,0:T(8,128)}, f32[2048,1152]{1,0:T(8,128)}), (f32[2048,1152]{1,0:T(8,128)}, f32[2048,1152]{1,0:T(8,128)})) %all-reduce.12.cloned.1.call-update) | async-done | bytes 18874384 | tf_op jit(solution)/shard_map/psum | solution.py:137
  680.3 22.4 %fusion.7 = (f32[8,1152]{1,0:T(8,128)S(1)}, f32[8,1152]{1,0:T(8,128)S(1)}, f32[8,1152]{1,0:T(8,128)S(1)}, f32[8,1152]{1,0:T(8,128)S(1)}, f32[8,1152]{1,0:T(8,128...) fusion(f32[2048,1152]{1,0:T(8,128)} %all-reduce.10.cloned.1.call-done, f32[2048,1152]{1,0:T(8,128)} %all-reduce.8.cloned.1.call-done, ...), kind=kLoop, calls=%fused_computation.17 | loop fusion | flops 61286400 | bytes 56976384 | tf_op jit(solution)/shard_map/reduce_sum | solution.py:157
  702.7 3.8 fusion.37
  706.6 4.6 copy.123
  711.2 5.8 fusion.21
  717.2 1.8 slice_reduce_fusion.1
  719.3 7.0 fusion.8
  726.3 11.0 fusion.2
  737.4 11.9 %multiply_add_fusion = f32[2048,1152]{1,0:T(8,128)} fusion(f32[2048,1152]{1,0:T(8,128)} %get-tuple-element.52, f32[2048,1152]{1,0:T(8,128)} %get-tuple-element.31, bf16[2048,1152]{1,0:T(8,128)(2,1)} %param.17, f32[2048]{0:T(1024)S(1)} %broadcast_multiply_fusion.1, f32[2048]{0:T(1024)S(1)} %broadcast_multiply_fusion.2, f32[2048]{0:T(1024)S(1)} %copy-done.30, ...), kind=kLoop, calls=%fused_computation.24 | loop fusion | flops 21233664 | bytes 33099776 | tf_op jit(solution)/shard_map/add | solution.py:212
  749.4 26.8 %all-reduce.1 = (f32[6,144]{1,0:T(8,128)}, f32[2,144]{1,0:T(2,128)}, f32[1152]{0:T(1024)}, f32[576]{0:T(1024)}, f32[1152]{0:T(1024)}, /*index=5*/f32[1152,2,2]{0,2,1:T(2,128)}, f32[2,2]{1,0:T(2,128)}) all-reduce(f32[6,144]{1,0:T(8,128)S(1)} %dynamic-slice_reduce_fusion, ...), channel_id=1, replica_groups=mesh['dp'=4,'tensor'=8] {'dp'}, use_global_device_ids=true, to_apply=%region_23.24 | all-reduce | flops 8644 | bytes 69152 | tf_op jit(solution)/shard_map/psum | solution.py:238
  776.2 341.5 %all-reduce.14.cloned.1.call-done = (f32[1152,6,144]{0,2,1:T(8,128)}, f32[1152,3,144]{0,2,1:T(8,128)}, f32[144,1152]{1,0:T(8,128)}, f32[1152,576]{0,1:T(8,128)}, f32[576,1152]{1,0:T(8,128)}) async-done(((f32[1152,6,144]{0,2,1:T(8,128)}, f32[1152,3,144]{0,2,1:T(8,128)}, f32[144,1152]{1,0:T(8,128)}, f32[1152,576]{0,1:T(8,128)}, f32[576,1152]{1,0:T(8,128)}), (f32[1152,6,144]{0,2,1:T(8,128)}, ...) | async-done | bytes 11943952 | tf_op jit(solution)/shard_map/psum | solution.py:238
  1117.7 4.5 copy.141
  1124.3 1.5 copy.144
  (195 shorter events, 22.8 us)
Async XLA Ops:
  7.2 7.6 copy-start
  7.2 7.0 copy-start.37
  7.2 7.6 copy-start.25
  7.2 221.2 %all-reduce.8.cloned.1.call-start = ((), (), s32[]{:S(2)}) async-start(), calls=%async_computation | async-start | bytes 18874368 | tf_op jit(solution)/shard_map/psum | solution.py:116
  10.4 34.5 %copy-start.27 = (f32[2048]{0:T(1024)}, f32[2048]{0:T(1024)S(1)}, u32[]{:S(2)}) copy-start(f32[2048]{0:T(1024)S(1)} %broadcast_multiply_fusion.6) | copy-start | bytes 24580
  67.0 6.8 copy-start.48
  78.8 2.7 copy-start.9
  79.5 2.8 copy-start.35
  79.6 2.7 copy-start.33
  81.5 2.8 copy-start.3
  84.6 5.4 copy-start.7
  90.0 313.8 %all-reduce.10.cloned.1.call-start = ((), (), s32[]{:S(2)}) async-start(), calls=%async_computation.1 | async-start | bytes 18874368 | tf_op jit(solution)/shard_map/psum | solution.py:153
  102.5 6.8 copy-start.23
  109.3 4.6 copy-start.47
  113.9 5.1 copy-start.11
  238.7 6.4 copy-start.2
  238.8 8.6 slice-start.2
  238.8 8.7 slice-start.4
  245.1 2.8 slice-start.5
  245.1 3.2 copy-start.46
  247.3 9.9 copy-start.13
  265.7 414.6 %all-reduce.12.cloned.1.call-start = ((), (), s32[]{:S(2)}) async-start(), calls=%async_computation.2 | async-start | bytes 37748736 | tf_op jit(solution)/shard_map/psum | solution.py:137
  403.8 9.1 copy-start.5
  412.9 10.7 copy-start.12
  423.6 4.9 copy-start.6
  423.6 3.9 copy-start.4
  428.5 3.9 copy-start.16
  440.1 8.6 slice-start
  440.1 677.6 %all-reduce.14.cloned.1.call-start = ((), (), s32[]{:S(2)}) async-start(), calls=%async_computation.3 | async-start | bytes 23887872 | tf_op jit(solution)/shard_map/psum | solution.py:238
  440.8 7.9 slice-start.1
  440.8 7.9 copy-start.54
  448.7 4.8 copy-start.8
  453.5 4.3 copy-start.17
  453.5 4.3 copy-start.19
  680.3 22.5 %copy-start.26 = (f32[8,1152]{1,0:T(8,128)S(1)}, f32[8,1152]{1,0:T(8,128)}, u32[]{:S(2)}) copy-start(f32[8,1152]{1,0:T(8,128)} %param.18) | copy-start | bytes 110596
  711.1 6.0 copy-start.32
  711.1 7.9 copy-start.43
  711.1 7.9 copy-start.44
  711.2 8.1 copy-start.28
  711.2 8.1 copy-start.30
  719.3 7.0 copy-start.24
  737.3 12.0 %copy-start.31 = (f32[1152]{0:T(1024)S(1)}, f32[1152]{0:T(1024)}, u32[]{:S(2)}) copy-start(f32[1152]{0:T(1024)} %get-tuple-element.46) | copy-start | bytes 13828
  737.3 12.0 %copy-start.40 = (f32[576]{0:T(1024)S(1)}, f32[576]{0:T(1024)}, u32[]{:S(2)}) copy-start(f32[576]{0:T(1024)} %get-tuple-element.58) | copy-start | bytes 6916
  1117.7 4.5 copy-start.20
  1117.7 5.8 copy-start.22
  1117.7 6.6 copy-start.15
  1122.2 3.6 copy-start.14
  1123.5 3.9 copy-start.1
  (18 other events, 24.6 us)
Sparse Core Ops, SparseCore 0:
  90.1 138.1 all-reduce.7
  265.8 137.9 all-reduce.9
  440.2 240.0 all-reduce.11
  706.7 410.9 all-reduce.13
where the time goes:
time: 1140 us; the launch traced here: 1130 us
  waiting for transfers between devices  788 us (69%)
  other arithmetic  112 us (10%)
  matrix products  84.5 us (7%)
  local copies, waits for them, and re-layouts  78.5 us (7%)
  blocking collectives  55.9 us (5%)
  between operations  14.9 us (1%)
    psum x1, waiting for transfers between devices, body(): lax.psum((modulate_weight_grad, modulate_bias_grad, input_weight_grad, in...  341 us
    psum x1, waiting for transfers between devices, body(): lax.psum(mlp_part, 'tensor') + reduce_bias.astype(jnp.float32)  216 us
    psum x1, waiting for transfers between devices, body(): lax.psum(hidden_two_part, 'tensor')  128 us
    psum x1, waiting for transfers between devices, body(): lax.psum(attention_part, 'tensor') + output_bias.astype(jnp.float32)  102 us
    unnamed x144, local copies, waits for them, and re-layouts  51.7 us
    all_gather x1, blocking collectives, body(): modulation = lax.all_gather(modulate_part, 'tensor', axis=2, tiled=True)  29.1 us
    psum x1, blocking collectives, body(): lax.psum((modulate_weight_grad, modulate_bias_grad, input_weight_grad, in...  26.8 us
  transfers between devices with their start and end apart: 4, of which 4 were waited for; matrix products, arithmetic and copies ran while one was open for 10% of the time, Pallas kernels for 0%

commit v1 on v0

--- a/solution.py
+++ b/solution.py
@@ -150,7 +150,7 @@
     expand_bias_grad = jnp.sum(expanded_grad.astype(jnp.float32), axis=0)
     expand_weight_grad = contract_rows(hidden_two, expanded_grad)
     hidden_two_part = contract_cols(expanded_grad, expand_weight)
-    hidden_two_grad = lax.psum(hidden_two_part, "tensor").reshape(
+    hidden_two_grad = jnp.sum(lax.all_gather(hidden_two_part, "tensor"), axis=0).reshape(
         item_count, item_length, model_width
     )
     shift_two_grad = jnp.sum(hidden_two_grad, axis=1)

time: 1140 us -> 1370 us (1.20)
  waiting for transfers between devices: 788 us -> 987 us
  other arithmetic: 112 us -> 136 us
    all_gather x0 -> x1, waiting for transfers between devices: none -> 326 us  [body(): lax.all_gather(hidden_two_part, 'tensor')]
    psum x1 -> x0, waiting for transfers between devices: 128 us -> none  [body(): lax.psum(hidden_two_part, 'tensor')]
    reduce_sum x0 -> x2, other arithmetic: none -> 35.4 us  [the longest x1 27.9 us: body(): jnp.sum(lax.all_gather(hidden_two_part, 'tensor'), axis=0)]
    unnamed x144 -> x159, local copies, waits for them, and re-layouts: 51.7 us -> 54.9 us
  transfers between devices with their start and end apart: 4 -> 4, of which waited for: 4 -> 4; matrix products, arithmetic and copies ran while one was open for 10% -> 8% of each run, Pallas kernels for 0% -> 0%
where the time goes in v1:
time: 1370 us; the launch traced here: 1360 us
  waiting for transfers between devices  987 us (72%)
  other arithmetic  136 us (10%)
  matrix products  86.9 us (6%)
  local copies, waits for them, and re-layouts  81.5 us (6%)
  blocking collectives  55.9 us (4%)
  between operations  15.2 us (1%)
    psum x1, waiting for transfers between devices, body(): lax.psum((modulate_weight_grad, modulate_bias_grad, input_weight_grad, in...  341 us
    all_gather x1, waiting for transfers between devices, body(): lax.all_gather(hidden_two_part, 'tensor')  326 us
    psum x1, waiting for transfers between devices, body(): lax.psum(mlp_part, 'tensor') + reduce_bias.astype(jnp.float32)  216 us
    psum x1, waiting for transfers between devices, body(): lax.psum(attention_part, 'tensor') + output_bias.astype(jnp.float32)  103 us
    unnamed x159, local copies, waits for them, and re-layouts  54.9 us
    all_gather x1, blocking collectives, body(): modulation = lax.all_gather(modulate_part, 'tensor', axis=2, tiled=True)  29 us
    reduce_sum x1, other arithmetic, body(): jnp.sum(lax.all_gather(hidden_two_part, 'tensor'), axis=0)  27.9 us
  transfers between devices with their start and end apart: 4, of which 4 were waited for; matrix products, arithmetic and copies ran while one was open for 8% of the time, Pallas kernels for 0%

profile of v1, /device:TPU:0, one launch (start us, length us, event | category | flops | bytes accessed | tf_op | source)
XLA Modules:
  0.0 1362.4 jit_solution(10994043278582130933)
XLA Ops:
  7.3 3.2 convert_reduce_fusion.2
  13.6 29.0 %all_gather.9 = f32[8,6,1152]{1,0,2:T(8,128)} all-gather(f32[8,6,144]{1,0,2:T(8,128)S(1)} %copy.78), channel_id=1, replica_groups=mesh['dp'=4,'tensor'=8] {'tensor'}, dimensions={2}, use_global_device_ids=true | all-gather | bytes 248832 | tf_op jit(solution)/shard_map/all_gather | solution.py:72
  42.6 21.9 %fusion.64 = (f32[8,1,1152]{1,0,2:T(8,128)}, f32[8,1,1152]{1,0,2:T(8,128)}, f32[8,1,1152]{1,0,2:T(8,128)}, f32[8,1,1152]{1,0,2:T(8,128)}, f32[8,1,1152]{1,0,2:T(8,128)}, /*index=5*/f32[8,1,1152]{1,0,2:T(8,128)}) fusion(f32[8,6,1152]{1,0,2:T(8,128)} %all_gather.9), kind=kLoop, calls=%fused_computation.136 | loop fusion | bytes 442368 | tf_op jit(solution)/shard_map/slice | solution.py:74
  64.5 3.4 copy.113
  68.0 3.3 copy.114
  72.0 4.9 fusion.16
  80.4 2.0 multiply_convert_fusion.3
  82.8 5.3 fusion.70
  88.4 3.3 copy.112
  91.7 3.3 copy.116
  95.1 3.3 copy.117
  98.4 3.4 copy.115
  101.9 4.5 convert_reduce_fusion
  106.5 4.9 broadcast_multiply_fusion
  111.4 2.7 copy.90
  114.1 4.4 copy.122
  118.9 4.4 copy.121
  123.3 103.2 %all-reduce.7.cloned.1.call-done = f32[2048,1152]{1,0:T(8,128)} async-done(((f32[2048,1152]{1,0:T(8,128)}), f32[2048,1152]{1,0:T(8,128)}) %all-reduce.7.cloned.1.call-update) | async-done | bytes 9437200 | tf_op jit(solution)/shard_map/psum | solution.py:116
  226.5 10.4 fusion.62
  236.9 4.9 multiply_reduce_fusion.4
  243.3 2.2 fusion.5
  246.5 9.3 multiply_convert_fusion
  257.2 6.6 fusion.72
  263.9 13.1 fusion.71
  277.0 326.3 %all-gather.3.cloned.1.call-done = f32[16384,1152]{1,0:T(8,128)} async-done(((f32[2048,1152]{1,0:T(8,128)}), f32[16384,1152]{1,0:T(8,128)}) %all-gather.3.cloned.1.call-update) | async-done | bytes 75497488 | tf_op jit(solution)/shard_map/all_gather | solution.py:153
  603.2 27.9 %reduce_sum.241 = f32[2048,1152]{1,0:T(8,128)} reduce(f32[8,2048,1152]{2,1,0:T(8,128)} %bitcast.28, f32[]{:T(128)} %constant.16.clone.1), dimensions={0}, to_apply=%region_8.9 | reduce | flops 16515072 | bytes 84934656 | tf_op jit(solution)/shard_map/reduce_sum | solution.py:153
  631.1 7.5 multiply_reduce_fusion.3
  643.1 8.6 convert_reduce_fusion.1
  651.7 2.0 multiply_reduce_fusion.9
  653.6 1.9 copy-done.6
  660.4 2.1 fusion.55
  662.7 5.4 convolution_bitcast_fusion
  668.8 7.9 fusion.75
  676.8 4.7 fusion.74
  681.6 4.3 fusion.73
  685.9 6.6 fusion.21
  692.4 215.7 %all-reduce.9.cloned.1.call-done = (f32[2048,1152]{1,0:T(8,128)}, f32[2048,1152]{1,0:T(8,128)}) async-done(((f32[2048,1152]{1,0:T(8,128)}, f32[2048,1152]{1,0:T(8,128)}), (f32[2048,1152]{1,0:T(8,128)}, f32[2048,1152]{1,0:T(8,128)})) %all-reduce.9.cloned.1.call-update) | async-done | bytes 18874384 | tf_op jit(solution)/shard_map/psum | solution.py:137
  908.2 22.5 %fusion.7 = (f32[8,1152]{1,0:T(8,128)S(1)}, f32[8,1152]{1,0:T(8,128)S(1)}, f32[8,1152]{1,0:T(8,128)S(1)}, f32[8,1152]{1,0:T(8,128)S(1)}, f32[8,1152]{1,0:T(8,128...) fusion(f32[2048,1152]{1,0:T(8,128)} %reduce_sum.241, f32[2048,1152]{1,0:T(8,128)} %all-reduce.7.cloned.1.call-done, ...), kind=kLoop, calls=%fused_computation.18 | loop fusion | flops 61286400 | bytes 56976384 | tf_op jit(solution)/shard_map/reduce_sum | solution.py:157
  930.8 3.8 fusion.36
  934.6 4.6 copy.124
  939.2 5.8 fusion.20
  945.2 1.8 slice_reduce_fusion.1
  947.3 7.0 fusion.8
  954.3 11.0 fusion.2
  965.4 11.9 multiply_add_fusion
  977.4 26.9 %all-reduce.1 = (f32[6,144]{1,0:T(8,128)}, f32[2,144]{1,0:T(2,128)}, f32[1152]{0:T(1024)}, f32[576]{0:T(1024)}, f32[1152]{0:T(1024)}, /*index=5*/f32[1152,2,2]{0,2,1:T(2,128)}, f32[2,2]{1,0:T(2,128)}) all-reduce(f32[6,144]{1,0:T(8,128)S(1)} %dynamic-slice_reduce_fusion, ...), channel_id=1, replica_groups=mesh['dp'=4,'tensor'=8] {'dp'}, use_global_device_ids=true, to_apply=%region_23.24 | all-reduce | flops 8644 | bytes 69152 | tf_op jit(solution)/shard_map/psum | solution.py:238
  1004.3 341.5 %all-reduce.11.cloned.1.call-done = (f32[1152,6,144]{0,2,1:T(8,128)}, f32[1152,3,144]{0,2,1:T(8,128)}, f32[144,1152]{1,0:T(8,128)}, f32[1152,576]{0,1:T(8,128)}, f32[576,1152]{1,0:T(8,128)}) async-done(((f32[1152,6,144]{0,2,1:T(8,128)}, f32[1152,3,144]{0,2,1:T(8,128)}, f32[144,1152]{1,0:T(8,128)}, f32[1152,576]{0,1:T(8,128)}, f32[576,1152]{1,0:T(8,128)}), (f32[1152,6,144]{0,2,1:T(8,128)}, ...) | async-done | bytes 11943952 | tf_op jit(solution)/shard_map/psum | solution.py:238
  1345.8 4.5 copy.141
  (212 shorter events, 28.0 us)
Async XLA Ops:
  7.2 5.4 copy-start
  7.2 5.4 copy-start.41
  7.2 219.3 %all-reduce.7.cloned.1.call-start = ((), (), s32[]{:S(2)}) async-start(), calls=%async_computation | async-start | bytes 18874368 | tf_op jit(solution)/shard_map/psum | solution.py:116
  7.3 3.9 copy-start.4
  7.3 5.3 copy-start.26
  11.1 31.5 %copy-start.30 = (f32[2048]{0:T(1024)}, f32[2048]{0:T(1024)S(1)}, u32[]{:S(2)}) copy-start(f32[2048]{0:T(1024)S(1)} %broadcast_multiply_fusion.6) | copy-start | bytes 24580
  12.6 58.8 %copy-start.37 = (f32[8,256]{1,0:T(8,128)}, f32[8,256]{1,0:T(8,128)S(1)}, u32[]{:S(2)}) copy-start(f32[8,256]{1,0:T(8,128)S(1)} %div.41) | copy-start | bytes 24580
  64.5 7.4 copy-start.52
  82.8 5.4 copy-start.8
  88.2 515.1 %all-gather.3.cloned.1.call-start = ((), (), s32[]{:S(2)}) async-start(), calls=%async_computation.1 | async-start | bytes 84934656 | tf_op jit(solution)/shard_map/all_gather | solution.py:153
  101.8 4.6 copy-start.24
  101.9 4.5 copy-start.51
  106.5 4.9 copy-start.12
  118.9 4.4 copy-start.45
  236.9 6.4 copy-start.2
  236.9 8.6 slice-start.5
  236.9 8.7 slice-start.7
  245.5 10.3 copy-start.14
  263.8 644.3 %all-reduce.9.cloned.1.call-start = ((), (), s32[]{:S(2)}) async-start(), calls=%async_computation.2 | async-start | bytes 37748736 | tf_op jit(solution)/shard_map/psum | solution.py:137
  631.1 9.1 copy-start.3
  631.1 10.3 slice-start
  631.1 11.5 slice-start.1
  643.1 8.6 copy-start.13
  651.7 5.2 copy-start.7
  651.7 3.9 copy-start.6
  668.1 8.6 slice-start.3
  668.1 677.6 %all-reduce.11.cloned.1.call-start = ((), (), s32[]{:S(2)}) async-start(), calls=%async_computation.3 | async-start | bytes 23887872 | tf_op jit(solution)/shard_map/psum | solution.py:238
  668.8 7.9 slice-start.4
  668.8 7.9 copy-start.58
  676.7 4.8 copy-start.9
  681.5 4.3 copy-start.18
  681.5 4.3 copy-start.20
  681.5 4.3 copy-start.29
  681.5 4.3 copy-start.35
  681.5 4.3 copy-start.38
  681.5 4.3 copy-start.40
  908.2 22.6 %copy-start.27 = (f32[8,1152]{1,0:T(8,128)S(1)}, f32[8,1152]{1,0:T(8,128)}, u32[]{:S(2)}) copy-start(f32[8,1152]{1,0:T(8,128)} %param.18) | copy-start | bytes 110596
  939.2 7.9 copy-start.47
  939.2 7.9 copy-start.48
  939.2 8.1 copy-start.31
  939.2 8.1 copy-start.33
  947.3 7.0 copy-start.25
  965.4 12.0 copy-start.36
  965.4 12.0 copy-start.44
  1345.8 4.5 copy-start.21
  1345.8 5.8 copy-start.23
  1345.8 6.6 copy-start.16
  1351.5 3.9 copy-start.1
  (25 other events, 52.9 us)
Sparse Core Ops, SparseCore 0:
  88.3 138.2 all-reduce.6
  263.9 339.2 all-gather.2
  668.2 239.8 all-reduce.8
  934.7 410.9 all-reduce.10
